TPU v7x, 512 devices: a whole 4x8x8 slice. The times are simulated.
512 devices in a mesh: cuts: 16 (over y, z_hi), slab: 32 (over x, z_lo, core).
Axes of the slice: x: 4, y: 8, z: 8 (z_hi: 2, z_lo: 4; z = z_hi * 4 + z_lo), core: 2. Of those that a mesh axis runs over, the one named last changes fastest.
Arguments:
- states: float32 [16, 64, 256, 128], P(None, 'slab', 'cuts'), may hold values from -4 to 4
- diffusivity: float32 [64, 256, 128], P('slab'), may hold values from 0.04 to 0.08
- coarse_gain: float32 [64, 256, 128], P('slab'), may hold values from 0.2 to 0.99
- read_block: int32 [16, 16, 2], replicated, may hold values from 0 to 63
- read_count: int32 [16, 16], replicated, may hold values from 0 to 2, as said below
Outputs:
- new_states: float32 [16, 64, 256, 128], P(None, 'slab', 'cuts')
- fetched_blocks: float32 [16, 16, 2, 64, 4, 128], P('cuts', None, None, 'slab')
Inputs may be any that keep to these rules, and one draw needn't show every extreme that they name: `read_block`: block ids count in units of 4 y rows. Slots of read_block at or beyond read_count[d, s] are not read. In every draw some slice d reads 2 blocks from every slice.
All inputs are finite; a program needn't handle non-finite values.
Results may differ from a plain program's by a relative error of at most 0.00002.
Values sent between devices are 32-bit elements; how exact they have to be, the bound alone decides.
No kernel may reach another device: no remote copies, remote signals or barrier semaphores. Data moves between devices by JAX's collectives and lax.ppermute only.
A program may use at most 64 MiB of HBM per device.

v0:
```python
import jax
import jax.numpy as jnp
from jax import lax
from jax.sharding import PartitionSpec as P

FINE = 8
BY = 4
courant = 0.45


def with_halo(block, sides, width):
    for axis, dim in sides:
        count = lax.axis_size(axis)
        forward = [(i, i + 1) for i in range(count - 1)]
        backward = [(target, source) for source, target in forward]
        low = lax.ppermute(
            lax.slice_in_dim(block, block.shape[dim] - width, None, axis=dim), axis, forward
        )
        high = lax.ppermute(lax.slice_in_dim(block, 0, width, axis=dim), axis, backward)
        block = jnp.concatenate([low, block, high], axis=dim)
    return block


def entering(value, axis, join, neutral):
    count, mine = (lax.axis_size(axis), lax.axis_index(axis))
    pieces = jax.tree.map(lambda part: lax.all_gather(part, axis), value)
    subtotal = jax.tree.map(
        lambda part, zero: jnp.full_like(part, 0) + jnp.asarray(zero, part.dtype), value, neutral
    )

    def turn(position, subtotal):
        longer = join(subtotal, jax.tree.map(lambda part: part[position], pieces))
        return jax.tree.map(lambda new, old: jnp.where(position < mine, new, old), longer, subtotal)

    return lax.fori_loop(0, count - 1, turn, subtotal)


def face_values(kappa_ext):
    face_z = 0.5 * (kappa_ext[1:] + kappa_ext[:-1])
    pad_y = jnp.pad(kappa_ext, ((0, 0), (1, 1), (0, 0)))
    face_y = 0.5 * (pad_y[:, 1:] + pad_y[:, :-1])
    pad_x = jnp.pad(kappa_ext, ((0, 0), (0, 0), (1, 1)))
    face_x = 0.5 * (pad_x[:, :, 1:] + pad_x[:, :, :-1])
    return (face_z, face_y, face_x)


def fine_step(field, face_z, face_y, face_x):
    centre = field[1:-1]
    upper_z = field[2:]
    lower_z = field[:-2]
    flux_sum = face_z[1:] * (upper_z - centre) + face_z[:-1] * (lower_z - centre)
    pad_y = jnp.pad(centre, ((0, 0), (1, 1), (0, 0)))
    faces_y = face_y[1:-1]
    flux_sum = (
        flux_sum
        + faces_y[:, 1:] * (pad_y[:, 2:] - centre)
        + faces_y[:, :-1] * (pad_y[:, :-2] - centre)
    )
    pad_x = jnp.pad(centre, ((0, 0), (0, 0), (1, 1)))
    faces_x = face_x[1:-1]
    flux_sum = (
        flux_sum
        + faces_x[:, :, 1:] * (pad_x[:, :, 2:] - centre)
        + faces_x[:, :, :-1] * (pad_x[:, :, :-2] - centre)
    )
    return centre + flux_sum - courant * (centre - lower_z)


def combine(earlier, later):
    return (earlier[0] * later[0], later[0] * earlier[1] + later[1])


def body(states, diffusivity, coarse_gain, read_block, read_count):
    position = lax.axis_index("cuts")
    layers = diffusivity.shape[0]
    y_rows = diffusivity.shape[1]
    slice_start = lax.all_to_all(states, "cuts", split_axis=0, concat_axis=2, tiled=True)[0]
    halo_depth = 1
    kappa_ext = with_halo(diffusivity, (("slab", 0),), halo_depth)
    face_z, face_y, face_x = face_values(kappa_ext)

    def single_step(step_index, current):
        padded = with_halo(current, (("slab", 0),), 1)
        return fine_step(padded, face_z, face_y, face_x)

    fine_end = lax.fori_loop(0, FINE, single_step, slice_start)
    difference = fine_end - coarse_gain * slice_start
    blocks = fine_end.reshape(layers, y_rows // BY, BY, fine_end.shape[2]).transpose(1, 0, 2, 3)
    wanted_blocks = lax.dynamic_index_in_dim(read_block, position, 1, keepdims=False)
    counts = lax.dynamic_index_in_dim(read_count, position, 1, keepdims=False)
    picked = jnp.take(blocks, wanted_blocks, axis=0)
    live_slot = jnp.arange(read_block.shape[2], dtype=jnp.int32)[None, :] < counts[:, None]
    picked = jnp.where(live_slot[:, :, None, None, None], picked, 0.0)
    received = lax.all_to_all(picked, "cuts", split_axis=0, concat_axis=0, tiled=True)
    fetched_blocks = received[None]
    leading = position == 0
    factor = jnp.where(leading, 0.0, coarse_gain)
    offset = jnp.where(leading, difference + coarse_gain * slice_start, difference)
    identity = (jnp.ones_like(factor), jnp.zeros_like(offset))
    prefix_pair = entering((factor, offset), "cuts", combine, identity)
    newest = factor * prefix_pair[1] + offset
    new_states = lax.all_to_all(newest[None], "cuts", split_axis=2, concat_axis=0, tiled=True)
    return (new_states, fetched_blocks)


def solution(mesh):
    placed = (P(None, "slab", "cuts", None), P("slab", None, None), P("slab", None, None), P(), P())
    return jax.shard_map(
        body,
        mesh=mesh,
        in_specs=placed,
        out_specs=(P(None, "slab", "cuts", None), P("cuts", None, None, "slab", None, None)),
        check_vma=False,
    )
```

profile of v0, /device:TPU:2, one launch (start us, length us, event | category | flops | bytes accessed | tf_op | source)
XLA Modules:
  0.0 444.3 jit_solution(2078087062163330457)
XLA Ops:
  8.2 1.9 collective-permute-start.3
  10.1 15.7 %all-to-all-start = ((f32[16,2,16,128]{3,2,1,0:T(8,128)}), f32[16,2,16,128]{3,2,1,0:T(8,128)S(1)}, u32[]{:S(2)}, u32[]{:S(2)}) async-start(f32[16,2,16,128]{3,2,1,0:T(8,128)} %param.9), calls=%async_computation | async-start | bytes 524288 | tf_op jit(solution)/shard_map/all_to_all | solution.py:77
  25.8 6.1 %collective-permute-start.2 = (f32[1,256,128]{2,1,0:T(8,128)S(1)}, f32[1,256,128]{2,1,0:T(8,128)S(1)}, u32[]{:S(2)}, u32[]{:S(2)}) collective-permute-start(f32[1,256,128]{2,1,0:T(8,128)S(1)} %get-tuple-element.210), channel_id=1, source_target_pairs={{1,0},{2,1},{3,2},{4,3},{5,4},{6,5},{7,6},{8,7},{9,8},{10,9},{11,1... | collective-permute-start | bytes 393224 | tf_op jit(solution)/shard_map/ppermute | solution.py:19
  32.9 3.4 collective-permute-done.2
  37.9 4.8 %all-to-all-done = f32[16,2,16,128]{3,2,1,0:T(8,128)S(1)} async-done(((f32[16,2,16,128]{3,2,1,0:T(8,128)}), f32[16,2,16,128]{3,2,1,0:T(8,128)S(1)}, u32[]{:S(2)}, u32[]{:S(2)}) %all-to-all-start) | async-done | bytes 262176 | tf_op jit(solution)/shard_map/all_to_all | solution.py:77
  42.7 91.9 %while.26 = (s32[]{:T(128)}, f32[2,256,128]{2,1,0:T(8,128)S(1)}, f32[3,256,128]{2,1,0:T(8,128)S(1)}, f32[4,257,128]{2,1,0:T(8,128)S(1)}, f32[4,256,129]{2,1,0:T(8,128)S(1)}, /*index=5*/s32[]{:T(128)}) while((s32[]{:T(128)}, f32[2,256,128]{2,1,0:T(8,128)S(1)}, f32[3,256,128]{2,1,0:T(8,128)S(1)}, f32[4,257,128]{2,1,0:T(8,128)S(1)}, ...), condition=%wide.region_1.2_spmd, body=%wide.region_0.1_spmd.sunk | while | flops 1507330 | bytes 4456597 | solution.py:86
  42.8 2.7 collective-permute-start
  45.5 5.7 %collective-permute-start.1 = (f32[1,256,128]{2,1,0:T(8,128)S(1)}, f32[1,256,128]{2,1,0:T(8,128)S(1)}, u32[]{:S(2)}, u32[]{:S(2)}) collective-permute-start(f32[1,256,128]{2,1,0:T(8,128)S(1)} %get-tuple-element.271), channel_id=1, source_target_pairs={{1,0},{2,1},{3,2},{4,3},{5,4},{6,5},{7,6},{8,7},{9,8},{10,9},{11,1... | collective-permute-start | bytes 393224 | tf_op jit(solution)/shard_map/while/body/eval_jaxpr/ppermute | solution.py:19
  51.9 1.7 collective-permute-done.1
  54.0 1.9 collective-permute-start
  56.0 6.5 %collective-permute-start.1 = (f32[1,256,128]{2,1,0:T(8,128)S(1)}, f32[1,256,128]{2,1,0:T(8,128)S(1)}, u32[]{:S(2)}, u32[]{:S(2)}) collective-permute-start(f32[1,256,128]{2,1,0:T(8,128)S(1)} %get-tuple-element.271), channel_id=1, source_target_pairs={{1,0},{2,1},{3,2},{4,3},{5,4},{6,5},{7,6},{8,7},{9,8},{10,9},{11,1... | collective-permute-start | bytes 393224 | tf_op jit(solution)/shard_map/while/body/eval_jaxpr/ppermute | solution.py:19
  63.3 1.7 collective-permute-done.1
  65.4 1.9 collective-permute-start
  67.3 6.5 %collective-permute-start.1 = (f32[1,256,128]{2,1,0:T(8,128)S(1)}, f32[1,256,128]{2,1,0:T(8,128)S(1)}, u32[]{:S(2)}, u32[]{:S(2)}) collective-permute-start(f32[1,256,128]{2,1,0:T(8,128)S(1)} %get-tuple-element.271), channel_id=1, source_target_pairs={{1,0},{2,1},{3,2},{4,3},{5,4},{6,5},{7,6},{8,7},{9,8},{10,9},{11,1... | collective-permute-start | bytes 393224 | tf_op jit(solution)/shard_map/while/body/eval_jaxpr/ppermute | solution.py:19
  74.6 2.0 collective-permute-done.1
  77.0 1.9 collective-permute-start
  78.9 6.6 %collective-permute-start.1 = (f32[1,256,128]{2,1,0:T(8,128)S(1)}, f32[1,256,128]{2,1,0:T(8,128)S(1)}, u32[]{:S(2)}, u32[]{:S(2)}) collective-permute-start(f32[1,256,128]{2,1,0:T(8,128)S(1)} %get-tuple-element.271), channel_id=1, source_target_pairs={{1,0},{2,1},{3,2},{4,3},{5,4},{6,5},{7,6},{8,7},{9,8},{10,9},{11,1... | collective-permute-start | bytes 393224 | tf_op jit(solution)/shard_map/while/body/eval_jaxpr/ppermute | solution.py:19
  86.2 1.8 collective-permute-done.1
  88.4 1.9 collective-permute-start
  90.3 6.5 %collective-permute-start.1 = (f32[1,256,128]{2,1,0:T(8,128)S(1)}, f32[1,256,128]{2,1,0:T(8,128)S(1)}, u32[]{:S(2)}, u32[]{:S(2)}) collective-permute-start(f32[1,256,128]{2,1,0:T(8,128)S(1)} %get-tuple-element.271), channel_id=1, source_target_pairs={{1,0},{2,1},{3,2},{4,3},{5,4},{6,5},{7,6},{8,7},{9,8},{10,9},{11,1... | collective-permute-start | bytes 393224 | tf_op jit(solution)/shard_map/while/body/eval_jaxpr/ppermute | solution.py:19
  97.6 2.6 collective-permute-done.1
  100.6 1.9 collective-permute-start
  102.5 6.6 %collective-permute-start.1 = (f32[1,256,128]{2,1,0:T(8,128)S(1)}, f32[1,256,128]{2,1,0:T(8,128)S(1)}, u32[]{:S(2)}, u32[]{:S(2)}) collective-permute-start(f32[1,256,128]{2,1,0:T(8,128)S(1)} %get-tuple-element.271), channel_id=1, source_target_pairs={{1,0},{2,1},{3,2},{4,3},{5,4},{6,5},{7,6},{8,7},{9,8},{10,9},{11,1... | collective-permute-start | bytes 393224 | tf_op jit(solution)/shard_map/while/body/eval_jaxpr/ppermute | solution.py:19
  109.8 1.8 collective-permute-done.1
  112.0 1.9 collective-permute-start
  113.9 6.6 %collective-permute-start.1 = (f32[1,256,128]{2,1,0:T(8,128)S(1)}, f32[1,256,128]{2,1,0:T(8,128)S(1)}, u32[]{:S(2)}, u32[]{:S(2)}) collective-permute-start(f32[1,256,128]{2,1,0:T(8,128)S(1)} %get-tuple-element.271), channel_id=1, source_target_pairs={{1,0},{2,1},{3,2},{4,3},{5,4},{6,5},{7,6},{8,7},{9,8},{10,9},{11,1... | collective-permute-start | bytes 393224 | tf_op jit(solution)/shard_map/while/body/eval_jaxpr/ppermute | solution.py:19
  121.3 1.7 collective-permute-done.1
  123.4 1.9 collective-permute-start
  125.3 6.5 %collective-permute-start.1 = (f32[1,256,128]{2,1,0:T(8,128)S(1)}, f32[1,256,128]{2,1,0:T(8,128)S(1)}, u32[]{:S(2)}, u32[]{:S(2)}) collective-permute-start(f32[1,256,128]{2,1,0:T(8,128)S(1)} %get-tuple-element.271), channel_id=1, source_target_pairs={{1,0},{2,1},{3,2},{4,3},{5,4},{6,5},{7,6},{8,7},{9,8},{10,9},{11,1... | collective-permute-start | bytes 393224 | tf_op jit(solution)/shard_map/while/body/eval_jaxpr/ppermute | solution.py:19
  132.6 1.7 collective-permute-done.1
  138.5 6.1 %all-to-all-start.2 = ((f32[16,2,2,4,128]{4,3,2,1,0:T(4,128)}), f32[16,2,2,4,128]{4,3,2,1,0:T(4,128)S(1)}, u32[]{:S(2)}, u32[]{:S(2)}) async-start(f32[16,2,2,4,128]{4,3,2,1,0:T(4,128)} %select_select_fusion), calls=%async_computation.2 | async-start | bytes 262144 | tf_op jit(solution)/shard_map/all_to_all | solution.py:94
  144.6 121.9 %all-gather.5.cloned.1.call-done = f32[32,256,128]{2,1,0:T(8,128)} async-done(((f32[2,256,128]{2,1,0:T(8,128)}), f32[32,256,128]{2,1,0:T(8,128)}) %all-gather.5.cloned.1.call-update) | async-done | bytes 4194320 | tf_op jit(solution)/shard_map/all_gather | solution.py:26
  266.4 130.4 %all-gather.7.cloned.1.call-done = f32[32,256,128]{2,1,0:T(8,128)} async-done(((f32[2,256,128]{2,1,0:T(8,128)}), f32[32,256,128]{2,1,0:T(8,128)}) %all-gather.7.cloned.1.call-update) | async-done | bytes 4194320 | tf_op jit(solution)/shard_map/all_gather | solution.py:26
  396.8 19.1 %while.27 = (s32[]{:T(128)}, f32[2,256,128]{2,1,0:T(8,128)S(1)}, s32[]{:T(128)}, f32[16,2,256,128]{3,2,1,0:T(8,128)}, f32[16,2,256,128]{3,2,1,0:T(8,128)}, /*index=5*/s32[]{:T(128)}, s32[]{:T(128)}) while((s32[]{:T(128)}, f32[2,256,128]{2,1,0:T(8,128)S(1)}, s32[]{:T(128)}, f32[16,2,256,128]{3,2,1,0:T(8,128)}, ...), condition=%wide.region_3.4_spmd.clone, body=%wide.region_2.3_spmd.clone.sunk | while | flops 262148 | bytes 1048685 | solution.py:35
  398.1 1.2 fusion.28
  399.3 1.2 fusion.28
  400.6 1.2 fusion.28
  401.9 1.2 fusion.28
  403.2 1.2 fusion.28
  404.4 1.2 fusion.28
  405.7 1.2 fusion.28
  407.0 1.2 fusion.28
  408.2 1.2 fusion.28
  409.5 1.2 fusion.28
  410.8 1.2 fusion.28
  412.1 1.2 fusion.28
  416.8 4.4 all-to-all-start.1
  421.3 14.8 %all-to-all-done.1 = f32[1,2,256,128]{3,1,0,2:T(2,128)S(1)} async-done(((f32[1,2,256,128]{3,1,0,2:T(2,128)}), f32[1,2,256,128]{3,1,0,2:T(2,128)S(1)}, u32[]{:S(2)}, u32[]{:S(2)}) %all-to-all-start.1) | async-done | bytes 262176 | tf_op jit(solution)/shard_map/all_to_all | solution.py:102
  (79 shorter events, 22.4 us)
Async XLA Ops:
  7.2 129.1 %copy-start = (s32[16,16,2]{1,2,0:T(2,128)S(1)}, s32[16,16,2]{1,2,0:T(2,128)}, u32[]{:S(2)}) copy-start(s32[16,16,2]{1,2,0:T(2,128)} %param.12) | copy-start | bytes 6148
  8.2 23.7 %collective-permute-start.3 = (f32[1,256,128]{2,1,0:T(8,128)S(1)}, f32[1,256,128]{2,1,0:T(8,128)S(1)}, u32[]{:S(2)}, u32[]{:S(2)}) collective-permute-start(f32[1,256,128]{2,1,0:T(8,128)S(1)} %get-tuple-element.209), channel_id=1, source_target_pairs={{0,1},{1,2},{2,3},{3,4},{4,5},{5,6},{6,7},{7,8},{8,9},{9,10},{10,1... | collective-permute-start | bytes 393224 | tf_op jit(solution)/shard_map/ppermute | solution.py:16
  10.1 32.5 %all-to-all-start = ((f32[16,2,16,128]{3,2,1,0:T(8,128)}), f32[16,2,16,128]{3,2,1,0:T(8,128)S(1)}, u32[]{:S(2)}, u32[]{:S(2)}) async-start(f32[16,2,16,128]{3,2,1,0:T(8,128)} %param.9), calls=%async_computation | async-start | bytes 524288 | tf_op jit(solution)/shard_map/all_to_all | solution.py:77
  25.8 240.7 %all-gather.5.cloned.1.call-start = ((), (), s32[]{:S(2)}) async-start(), calls=%async_computation.3 | async-start | bytes 4456448 | tf_op jit(solution)/shard_map/all_gather | solution.py:26
  25.8 10.5 %collective-permute-start.2 = (f32[1,256,128]{2,1,0:T(8,128)S(1)}, f32[1,256,128]{2,1,0:T(8,128)S(1)}, u32[]{:S(2)}, u32[]{:S(2)}) collective-permute-start(f32[1,256,128]{2,1,0:T(8,128)S(1)} %get-tuple-element.210), channel_id=1, source_target_pairs={{1,0},{2,1},{3,2},{4,3},{5,4},{6,5},{7,6},{8,7},{9,8},{10,9},{11,1... | collective-permute-start | bytes 393224 | tf_op jit(solution)/shard_map/ppermute | solution.py:19
  42.7 92.0 %copy-start.3 = (f32[2,256,128]{2,1,0:T(8,128)S(1)}, f32[2,256,128]{2,1,0:T(8,128)}, u32[]{:S(2)}) copy-start(f32[2,256,128]{2,1,0:T(8,128)} %param.11) | copy-start | bytes 786436
  42.7 94.1 %copy-start.4 = (s32[16,16]{1,0:T(8,128)S(1)}, s32[16,16]{1,0:T(8,128)}, u32[]{:S(2)}) copy-start(s32[16,16]{1,0:T(8,128)} %param.13) | copy-start | bytes 3076
  42.8 9.2 %collective-permute-start = (f32[1,256,128]{2,1,0:T(8,128)S(1)}, f32[1,256,128]{2,1,0:T(8,128)S(1)}, u32[]{:S(2)}, u32[]{:S(2)}) collective-permute-start(f32[1,256,128]{2,1,0:T(8,128)S(1)} %get-tuple-element.270), channel_id=1, source_target_pairs={{0,1},{1,2},{2,3},{3,4},{4,5},{5,6},{6,7},{7,8},{8,9},{9,10},{10,1... | collective-permute-start | bytes 393224 | tf_op jit(solution)/shard_map/while/body/eval_jaxpr/ppermute | solution.py:16
  45.5 8.2 %collective-permute-start.1 = (f32[1,256,128]{2,1,0:T(8,128)S(1)}, f32[1,256,128]{2,1,0:T(8,128)S(1)}, u32[]{:S(2)}, u32[]{:S(2)}) collective-permute-start(f32[1,256,128]{2,1,0:T(8,128)S(1)} %get-tuple-element.271), channel_id=1, source_target_pairs={{1,0},{2,1},{3,2},{4,3},{5,4},{6,5},{7,6},{8,7},{9,8},{10,9},{11,1... | collective-permute-start | bytes 393224 | tf_op jit(solution)/shard_map/while/body/eval_jaxpr/ppermute | solution.py:19
  54.0 9.2 %collective-permute-start = (f32[1,256,128]{2,1,0:T(8,128)S(1)}, f32[1,256,128]{2,1,0:T(8,128)S(1)}, u32[]{:S(2)}, u32[]{:S(2)}) collective-permute-start(f32[1,256,128]{2,1,0:T(8,128)S(1)} %get-tuple-element.270), channel_id=1, source_target_pairs={{0,1},{1,2},{2,3},{3,4},{4,5},{5,6},{6,7},{7,8},{8,9},{9,10},{10,1... | collective-permute-start | bytes 393224 | tf_op jit(solution)/shard_map/while/body/eval_jaxpr/ppermute | solution.py:16
  56.0 9.0 %collective-permute-start.1 = (f32[1,256,128]{2,1,0:T(8,128)S(1)}, f32[1,256,128]{2,1,0:T(8,128)S(1)}, u32[]{:S(2)}, u32[]{:S(2)}) collective-permute-start(f32[1,256,128]{2,1,0:T(8,128)S(1)} %get-tuple-element.271), channel_id=1, source_target_pairs={{1,0},{2,1},{3,2},{4,3},{5,4},{6,5},{7,6},{8,7},{9,8},{10,9},{11,1... | collective-permute-start | bytes 393224 | tf_op jit(solution)/shard_map/while/body/eval_jaxpr/ppermute | solution.py:19
  65.4 9.3 %collective-permute-start = (f32[1,256,128]{2,1,0:T(8,128)S(1)}, f32[1,256,128]{2,1,0:T(8,128)S(1)}, u32[]{:S(2)}, u32[]{:S(2)}) collective-permute-start(f32[1,256,128]{2,1,0:T(8,128)S(1)} %get-tuple-element.270), channel_id=1, source_target_pairs={{0,1},{1,2},{2,3},{3,4},{4,5},{5,6},{6,7},{7,8},{8,9},{9,10},{10,1... | collective-permute-start | bytes 393224 | tf_op jit(solution)/shard_map/while/body/eval_jaxpr/ppermute | solution.py:16
  67.3 9.3 %collective-permute-start.1 = (f32[1,256,128]{2,1,0:T(8,128)S(1)}, f32[1,256,128]{2,1,0:T(8,128)S(1)}, u32[]{:S(2)}, u32[]{:S(2)}) collective-permute-start(f32[1,256,128]{2,1,0:T(8,128)S(1)} %get-tuple-element.271), channel_id=1, source_target_pairs={{1,0},{2,1},{3,2},{4,3},{5,4},{6,5},{7,6},{8,7},{9,8},{10,9},{11,1... | collective-permute-start | bytes 393224 | tf_op jit(solution)/shard_map/while/body/eval_jaxpr/ppermute | solution.py:19
  77.0 9.2 %collective-permute-start = (f32[1,256,128]{2,1,0:T(8,128)S(1)}, f32[1,256,128]{2,1,0:T(8,128)S(1)}, u32[]{:S(2)}, u32[]{:S(2)}) collective-permute-start(f32[1,256,128]{2,1,0:T(8,128)S(1)} %get-tuple-element.270), channel_id=1, source_target_pairs={{0,1},{1,2},{2,3},{3,4},{4,5},{5,6},{6,7},{7,8},{8,9},{9,10},{10,1... | collective-permute-start | bytes 393224 | tf_op jit(solution)/shard_map/while/body/eval_jaxpr/ppermute | solution.py:16
  78.9 9.1 %collective-permute-start.1 = (f32[1,256,128]{2,1,0:T(8,128)S(1)}, f32[1,256,128]{2,1,0:T(8,128)S(1)}, u32[]{:S(2)}, u32[]{:S(2)}) collective-permute-start(f32[1,256,128]{2,1,0:T(8,128)S(1)} %get-tuple-element.271), channel_id=1, source_target_pairs={{1,0},{2,1},{3,2},{4,3},{5,4},{6,5},{7,6},{8,7},{9,8},{10,9},{11,1... | collective-permute-start | bytes 393224 | tf_op jit(solution)/shard_map/while/body/eval_jaxpr/ppermute | solution.py:19
  88.4 9.2 %collective-permute-start = (f32[1,256,128]{2,1,0:T(8,128)S(1)}, f32[1,256,128]{2,1,0:T(8,128)S(1)}, u32[]{:S(2)}, u32[]{:S(2)}) collective-permute-start(f32[1,256,128]{2,1,0:T(8,128)S(1)} %get-tuple-element.270), channel_id=1, source_target_pairs={{0,1},{1,2},{2,3},{3,4},{4,5},{5,6},{6,7},{7,8},{8,9},{9,10},{10,1... | collective-permute-start | bytes 393224 | tf_op jit(solution)/shard_map/while/body/eval_jaxpr/ppermute | solution.py:16
  90.3 9.9 %collective-permute-start.1 = (f32[1,256,128]{2,1,0:T(8,128)S(1)}, f32[1,256,128]{2,1,0:T(8,128)S(1)}, u32[]{:S(2)}, u32[]{:S(2)}) collective-permute-start(f32[1,256,128]{2,1,0:T(8,128)S(1)} %get-tuple-element.271), channel_id=1, source_target_pairs={{1,0},{2,1},{3,2},{4,3},{5,4},{6,5},{7,6},{8,7},{9,8},{10,9},{11,1... | collective-permute-start | bytes 393224 | tf_op jit(solution)/shard_map/while/body/eval_jaxpr/ppermute | solution.py:19
  100.6 9.3 %collective-permute-start = (f32[1,256,128]{2,1,0:T(8,128)S(1)}, f32[1,256,128]{2,1,0:T(8,128)S(1)}, u32[]{:S(2)}, u32[]{:S(2)}) collective-permute-start(f32[1,256,128]{2,1,0:T(8,128)S(1)} %get-tuple-element.270), channel_id=1, source_target_pairs={{0,1},{1,2},{2,3},{3,4},{4,5},{5,6},{6,7},{7,8},{8,9},{9,10},{10,1... | collective-permute-start | bytes 393224 | tf_op jit(solution)/shard_map/while/body/eval_jaxpr/ppermute | solution.py:16
  102.5 9.1 %collective-permute-start.1 = (f32[1,256,128]{2,1,0:T(8,128)S(1)}, f32[1,256,128]{2,1,0:T(8,128)S(1)}, u32[]{:S(2)}, u32[]{:S(2)}) collective-permute-start(f32[1,256,128]{2,1,0:T(8,128)S(1)} %get-tuple-element.271), channel_id=1, source_target_pairs={{1,0},{2,1},{3,2},{4,3},{5,4},{6,5},{7,6},{8,7},{9,8},{10,9},{11,1... | collective-permute-start | bytes 393224 | tf_op jit(solution)/shard_map/while/body/eval_jaxpr/ppermute | solution.py:19
  112.0 9.3 %collective-permute-start = (f32[1,256,128]{2,1,0:T(8,128)S(1)}, f32[1,256,128]{2,1,0:T(8,128)S(1)}, u32[]{:S(2)}, u32[]{:S(2)}) collective-permute-start(f32[1,256,128]{2,1,0:T(8,128)S(1)} %get-tuple-element.270), channel_id=1, source_target_pairs={{0,1},{1,2},{2,3},{3,4},{4,5},{5,6},{6,7},{7,8},{8,9},{9,10},{10,1... | collective-permute-start | bytes 393224 | tf_op jit(solution)/shard_map/while/body/eval_jaxpr/ppermute | solution.py:16
  113.9 9.1 %collective-permute-start.1 = (f32[1,256,128]{2,1,0:T(8,128)S(1)}, f32[1,256,128]{2,1,0:T(8,128)S(1)}, u32[]{:S(2)}, u32[]{:S(2)}) collective-permute-start(f32[1,256,128]{2,1,0:T(8,128)S(1)} %get-tuple-element.271), channel_id=1, source_target_pairs={{1,0},{2,1},{3,2},{4,3},{5,4},{6,5},{7,6},{8,7},{9,8},{10,9},{11,1... | collective-permute-start | bytes 393224 | tf_op jit(solution)/shard_map/while/body/eval_jaxpr/ppermute | solution.py:19
  123.4 9.3 %collective-permute-start = (f32[1,256,128]{2,1,0:T(8,128)S(1)}, f32[1,256,128]{2,1,0:T(8,128)S(1)}, u32[]{:S(2)}, u32[]{:S(2)}) collective-permute-start(f32[1,256,128]{2,1,0:T(8,128)S(1)} %get-tuple-element.270), channel_id=1, source_target_pairs={{0,1},{1,2},{2,3},{3,4},{4,5},{5,6},{6,7},{7,8},{8,9},{9,10},{10,1... | collective-permute-start | bytes 393224 | tf_op jit(solution)/shard_map/while/body/eval_jaxpr/ppermute | solution.py:16
  125.3 9.0 %collective-permute-start.1 = (f32[1,256,128]{2,1,0:T(8,128)S(1)}, f32[1,256,128]{2,1,0:T(8,128)S(1)}, u32[]{:S(2)}, u32[]{:S(2)}) collective-permute-start(f32[1,256,128]{2,1,0:T(8,128)S(1)} %get-tuple-element.271), channel_id=1, source_target_pairs={{1,0},{2,1},{3,2},{4,3},{5,4},{6,5},{7,6},{8,7},{9,8},{10,9},{11,1... | collective-permute-start | bytes 393224 | tf_op jit(solution)/shard_map/while/body/eval_jaxpr/ppermute | solution.py:19
  135.5 280.4 %copy-start.1 = (f32[2,256,128]{2,1,0:T(8,128)S(1)}, f32[2,256,128]{2,1,0:T(8,128)}, u32[]{:S(2)}) copy-start(f32[2,256,128]{2,1,0:T(8,128)} %get-tuple-element.207) | copy-start | bytes 786436
  135.5 280.4 %copy-start.2 = (f32[2,256,128]{2,1,0:T(8,128)S(1)}, f32[2,256,128]{2,1,0:T(8,128)}, u32[]{:S(2)}) copy-start(f32[2,256,128]{2,1,0:T(8,128)} %get-tuple-element.208) | copy-start | bytes 786436
  135.5 261.3 %all-gather.7.cloned.1.call-start = ((), (), s32[]{:S(2)}) async-start(), calls=%async_computation.4 | async-start | bytes 4456448 | tf_op jit(solution)/shard_map/all_gather | solution.py:26
  138.5 278.3 %all-to-all-start.2 = ((f32[16,2,2,4,128]{4,3,2,1,0:T(4,128)}), f32[16,2,2,4,128]{4,3,2,1,0:T(4,128)S(1)}, u32[]{:S(2)}, u32[]{:S(2)}) async-start(f32[16,2,2,4,128]{4,3,2,1,0:T(4,128)} %select_select_fusion), calls=%async_computation.2 | async-start | bytes 262144 | tf_op jit(solution)/shard_map/all_to_all | solution.py:94
  416.8 19.2 %all-to-all-start.1 = ((f32[1,2,256,128]{3,1,0,2:T(2,128)}), f32[1,2,256,128]{3,1,0,2:T(2,128)S(1)}, u32[]{:S(2)}, u32[]{:S(2)}) async-start(f32[1,2,256,128]{3,1,0,2:T(2,128)} %copy.19), calls=%async_computation.1 | async-start | bytes 524288 | tf_op jit(solution)/shard_map/all_to_all | solution.py:102
Sparse Core Ops, SparseCore 0:
  135.6 130.7 all-gather.4
  269.6 127.1 all-gather.6
where the time goes:
time: 445 us; the launch traced here: 444 us
  waiting for transfers between devices  297 us (67%)
  starting transfers between devices  102 us (23%)
  other arithmetic  24.4 us (5%)
  between operations  14.3 us (3%)
  local copies, waits for them, and re-layouts  5.96 us (1%)
    all_gather x2, waiting for transfers between devices, entering(): pieces = jax.tree.map(lambda part: lax.all_gather(part, axis), value)  252 us
    ppermute x9, starting transfers between devices, with_halo(): lax.ppermute(lax.slice_in_dim(block, 0, width, axis=dim), axis, backward)  57.5 us
    select_n x15, other arithmetic, turn(): jnp.where(position < mine, new, old)  18.7 us
    ppermute x9, waiting for transfers between devices, with_halo(): lax.ppermute(lax.slice_in_dim(block, 0, width, axis=dim), axis, backward)  18.5 us
    ppermute x9, starting transfers between devices, with_halo(): lax.ppermute(lax.slice_in_dim(block, block.shape[dim] - width, None, axis...  18.1 us
    all_to_all x1, starting transfers between devices, body(): lax.all_to_all(states, 'cuts', split_axis=0, concat_axis=2, tiled=True)[0]  15.7 us
    all_to_all x1, waiting for transfers between devices, body(): lax.all_to_all(newest[None], 'cuts', split_axis=2, concat_axis=0, tiled=T...  14.8 us
  transfers between devices with their start and end apart: 23, of which 21 were waited for; matrix products, arithmetic and copies ran while one was open for 5% of the time, Pallas kernels for 0%

commit v1 on v0

--- a/solution.py
+++ b/solution.py
@@ -74,7 +74,10 @@
     position = lax.axis_index("cuts")
     layers = diffusivity.shape[0]
     y_rows = diffusivity.shape[1]
-    slice_start = lax.all_to_all(states, "cuts", split_axis=0, concat_axis=2, tiled=True)[0]
+    slice_start = jnp.concatenate(
+        lax.all_to_all(jnp.stack(jnp.split(states, lax.axis_size("cuts"), axis=0)), "cuts", 0, 0),
+        axis=2,
+    )[0]
     halo_depth = 1
     kappa_ext = with_halo(diffusivity, (("slab", 0),), halo_depth)
     face_z, face_y, face_x = face_values(kappa_ext)

time: 445 us -> 468 us (1.052)
  local copies, waits for them, and re-layouts: 5.96 us -> 27.1 us
    unnamed x15 -> x30, local copies, waits for them, and re-layouts: 2.42 us -> 22.3 us
  transfers between devices with their start and end apart: 23 -> 23, of which waited for: 21 -> 21; matrix products, arithmetic and copies ran while one was open for 5% -> 10% of each run, Pallas kernels for 0% -> 0%
where the time goes in v1:
time: 468 us; the launch traced here: 465 us
  waiting for transfers between devices  297 us (63%)
  starting transfers between devices  102 us (22%)
  local copies, waits for them, and re-layouts  27.1 us (6%)
  other arithmetic  24.4 us (5%)
  between operations  14.3 us (3%)
    all_gather x2, waiting for transfers between devices, entering(): pieces = jax.tree.map(lambda part: lax.all_gather(part, axis), value)  252 us
    ppermute x9, starting transfers between devices, with_halo(): lax.ppermute(lax.slice_in_dim(block, 0, width, axis=dim), axis, backward)  57.5 us
    unnamed x30, local copies, waits for them, and re-layouts  22.3 us
    select_n x15, other arithmetic, turn(): jnp.where(position < mine, new, old)  18.7 us
    ppermute x9, waiting for transfers between devices, with_halo(): lax.ppermute(lax.slice_in_dim(block, 0, width, axis=dim), axis, backward)  18.5 us
    ppermute x9, starting transfers between devices, with_halo(): lax.ppermute(lax.slice_in_dim(block, block.shape[dim] - width, None, axis...  18.1 us
    all_to_all x1, starting transfers between devices, body(): lax.all_to_all(jnp.stack(jnp.split(states, lax.axis_size('cuts'), axis=0)...  15.6 us
    all_to_all x1, waiting for transfers between devices, body(): lax.all_to_all(newest[None], 'cuts', split_axis=2, concat_axis=0, tiled=T...  14.8 us
  transfers between devices with their start and end apart: 23, of which 21 were waited for; matrix products, arithmetic and copies ran while one was open for 10% of the time, Pallas kernels for 0%

profile of v1, /device:TPU:2, one launch (start us, length us, event | category | flops | bytes accessed | tf_op | source)
XLA Modules:
  0.0 465.4 jit_solution(11347986394968924198)
XLA Ops:
  8.2 1.9 collective-permute-start.3
  10.1 1.3 constant_dynamic-update-slice_fusion.15
  11.4 1.3 constant_dynamic-update-slice_fusion.14
  12.8 1.3 constant_dynamic-update-slice_fusion.13
  14.1 1.3 constant_dynamic-update-slice_fusion.12
  15.4 1.3 constant_dynamic-update-slice_fusion.11
  16.7 1.3 constant_dynamic-update-slice_fusion.10
  18.0 1.3 constant_dynamic-update-slice_fusion.9
  19.4 1.3 constant_dynamic-update-slice_fusion.8
  26.0 1.3 constant_dynamic-update-slice_fusion.3
  27.3 1.3 constant_dynamic-update-slice_fusion.2
  28.6 1.3 constant_dynamic-update-slice_fusion.1
  30.0 1.3 constant_dynamic-update-slice_fusion
  31.3 15.6 %all-to-all-start = ((f32[16,1,2,16,128]{4,3,2,1,0:T(8,128)}), f32[16,1,2,16,128]{4,3,2,1,0:T(8,128)S(1)}, u32[]{:S(2)}, u32[]{:S(2)}) async-start(f32[16,1,2,16,128]{4,3,2,1,0:T(8,128)} %constant_dynamic-update-slice_fusion), calls=%async_computation | async-start | bytes 524288 | tf_op jit(solution)/shard_map/all_to_all | solution.py:78
  47.0 6.1 %collective-permute-start.2 = (f32[1,256,128]{2,1,0:T(8,128)S(1)}, f32[1,256,128]{2,1,0:T(8,128)S(1)}, u32[]{:S(2)}, u32[]{:S(2)}) collective-permute-start(f32[1,256,128]{2,1,0:T(8,128)S(1)} %get-tuple-element.210), channel_id=1, source_target_pairs={{1,0},{2,1},{3,2},{4,3},{5,4},{6,5},{7,6},{8,7},{9,8},{10,9},{11,1... | collective-permute-start | bytes 393224 | tf_op jit(solution)/shard_map/ppermute | solution.py:19
  54.1 3.4 collective-permute-done.2
  59.0 4.8 %all-to-all-done = f32[16,1,2,16,128]{4,3,2,1,0:T(8,128)S(1)} async-done(((f32[16,1,2,16,128]{4,3,2,1,0:T(8,128)}), f32[16,1,2,16,128]{4,3,2,1,0:T(8,128)S(1)}, u32[]{:S(2)}, u32[]{:S(2)}) %all-to-all-start) | async-done | bytes 262176 | tf_op jit(solution)/shard_map/all_to_all | solution.py:78
  63.9 91.9 %while.26 = (s32[]{:T(128)}, f32[2,256,128]{2,1,0:T(8,128)S(1)}, f32[3,256,128]{2,1,0:T(8,128)S(1)}, f32[4,257,128]{2,1,0:T(8,128)S(1)}, f32[4,256,129]{2,1,0:T(8,128)S(1)}, /*index=5*/s32[]{:T(128)}) while((s32[]{:T(128)}, f32[2,256,128]{2,1,0:T(8,128)S(1)}, f32[3,256,128]{2,1,0:T(8,128)S(1)}, f32[4,257,128]{2,1,0:T(8,128)S(1)}, ...), condition=%wide.region_1.2_spmd, body=%wide.region_0.1_spmd.sunk | while | flops 1507330 | bytes 4456597 | solution.py:89
  63.9 2.7 collective-permute-start
  66.7 5.7 %collective-permute-start.1 = (f32[1,256,128]{2,1,0:T(8,128)S(1)}, f32[1,256,128]{2,1,0:T(8,128)S(1)}, u32[]{:S(2)}, u32[]{:S(2)}) collective-permute-start(f32[1,256,128]{2,1,0:T(8,128)S(1)} %get-tuple-element.271), channel_id=1, source_target_pairs={{1,0},{2,1},{3,2},{4,3},{5,4},{6,5},{7,6},{8,7},{9,8},{10,9},{11,1... | collective-permute-start | bytes 393224 | tf_op jit(solution)/shard_map/while/body/eval_jaxpr/ppermute | solution.py:19
  73.1 1.7 collective-permute-done.1
  75.2 1.9 collective-permute-start
  77.1 6.5 %collective-permute-start.1 = (f32[1,256,128]{2,1,0:T(8,128)S(1)}, f32[1,256,128]{2,1,0:T(8,128)S(1)}, u32[]{:S(2)}, u32[]{:S(2)}) collective-permute-start(f32[1,256,128]{2,1,0:T(8,128)S(1)} %get-tuple-element.271), channel_id=1, source_target_pairs={{1,0},{2,1},{3,2},{4,3},{5,4},{6,5},{7,6},{8,7},{9,8},{10,9},{11,1... | collective-permute-start | bytes 393224 | tf_op jit(solution)/shard_map/while/body/eval_jaxpr/ppermute | solution.py:19
  84.4 1.7 collective-permute-done.1
  86.5 1.9 collective-permute-start
  88.5 6.5 %collective-permute-start.1 = (f32[1,256,128]{2,1,0:T(8,128)S(1)}, f32[1,256,128]{2,1,0:T(8,128)S(1)}, u32[]{:S(2)}, u32[]{:S(2)}) collective-permute-start(f32[1,256,128]{2,1,0:T(8,128)S(1)} %get-tuple-element.271), channel_id=1, source_target_pairs={{1,0},{2,1},{3,2},{4,3},{5,4},{6,5},{7,6},{8,7},{9,8},{10,9},{11,1... | collective-permute-start | bytes 393224 | tf_op jit(solution)/shard_map/while/body/eval_jaxpr/ppermute | solution.py:19
  95.8 2.0 collective-permute-done.1
  98.1 1.9 collective-permute-start
  100.1 6.6 %collective-permute-start.1 = (f32[1,256,128]{2,1,0:T(8,128)S(1)}, f32[1,256,128]{2,1,0:T(8,128)S(1)}, u32[]{:S(2)}, u32[]{:S(2)}) collective-permute-start(f32[1,256,128]{2,1,0:T(8,128)S(1)} %get-tuple-element.271), channel_id=1, source_target_pairs={{1,0},{2,1},{3,2},{4,3},{5,4},{6,5},{7,6},{8,7},{9,8},{10,9},{11,1... | collective-permute-start | bytes 393224 | tf_op jit(solution)/shard_map/while/body/eval_jaxpr/ppermute | solution.py:19
  107.4 1.8 collective-permute-done.1
  109.5 1.9 collective-permute-start
  111.4 6.5 %collective-permute-start.1 = (f32[1,256,128]{2,1,0:T(8,128)S(1)}, f32[1,256,128]{2,1,0:T(8,128)S(1)}, u32[]{:S(2)}, u32[]{:S(2)}) collective-permute-start(f32[1,256,128]{2,1,0:T(8,128)S(1)} %get-tuple-element.271), channel_id=1, source_target_pairs={{1,0},{2,1},{3,2},{4,3},{5,4},{6,5},{7,6},{8,7},{9,8},{10,9},{11,1... | collective-permute-start | bytes 393224 | tf_op jit(solution)/shard_map/while/body/eval_jaxpr/ppermute | solution.py:19
  118.7 2.6 collective-permute-done.1
  121.7 1.9 collective-permute-start
  123.7 6.6 %collective-permute-start.1 = (f32[1,256,128]{2,1,0:T(8,128)S(1)}, f32[1,256,128]{2,1,0:T(8,128)S(1)}, u32[]{:S(2)}, u32[]{:S(2)}) collective-permute-start(f32[1,256,128]{2,1,0:T(8,128)S(1)} %get-tuple-element.271), channel_id=1, source_target_pairs={{1,0},{2,1},{3,2},{4,3},{5,4},{6,5},{7,6},{8,7},{9,8},{10,9},{11,1... | collective-permute-start | bytes 393224 | tf_op jit(solution)/shard_map/while/body/eval_jaxpr/ppermute | solution.py:19
  131.0 1.8 collective-permute-done.1
  133.2 1.9 collective-permute-start
  135.1 6.6 %collective-permute-start.1 = (f32[1,256,128]{2,1,0:T(8,128)S(1)}, f32[1,256,128]{2,1,0:T(8,128)S(1)}, u32[]{:S(2)}, u32[]{:S(2)}) collective-permute-start(f32[1,256,128]{2,1,0:T(8,128)S(1)} %get-tuple-element.271), channel_id=1, source_target_pairs={{1,0},{2,1},{3,2},{4,3},{5,4},{6,5},{7,6},{8,7},{9,8},{10,9},{11,1... | collective-permute-start | bytes 393224 | tf_op jit(solution)/shard_map/while/body/eval_jaxpr/ppermute | solution.py:19
  142.5 1.7 collective-permute-done.1
  144.5 1.9 collective-permute-start
  146.5 6.5 %collective-permute-start.1 = (f32[1,256,128]{2,1,0:T(8,128)S(1)}, f32[1,256,128]{2,1,0:T(8,128)S(1)}, u32[]{:S(2)}, u32[]{:S(2)}) collective-permute-start(f32[1,256,128]{2,1,0:T(8,128)S(1)} %get-tuple-element.271), channel_id=1, source_target_pairs={{1,0},{2,1},{3,2},{4,3},{5,4},{6,5},{7,6},{8,7},{9,8},{10,9},{11,1... | collective-permute-start | bytes 393224 | tf_op jit(solution)/shard_map/while/body/eval_jaxpr/ppermute | solution.py:19
  153.8 1.7 collective-permute-done.1
  159.7 6.1 %all-to-all-start.2 = ((f32[16,2,2,4,128]{4,3,2,1,0:T(4,128)}), f32[16,2,2,4,128]{4,3,2,1,0:T(4,128)S(1)}, u32[]{:S(2)}, u32[]{:S(2)}) async-start(f32[16,2,2,4,128]{4,3,2,1,0:T(4,128)} %select_select_fusion), calls=%async_computation.2 | async-start | bytes 262144 | tf_op jit(solution)/shard_map/all_to_all | solution.py:97
  165.7 121.9 %all-gather.5.cloned.1.call-done = f32[32,256,128]{2,1,0:T(8,128)} async-done(((f32[2,256,128]{2,1,0:T(8,128)}), f32[32,256,128]{2,1,0:T(8,128)}) %all-gather.5.cloned.1.call-update) | async-done | bytes 4194320 | tf_op jit(solution)/shard_map/all_gather | solution.py:26
  287.6 130.4 %all-gather.7.cloned.1.call-done = f32[32,256,128]{2,1,0:T(8,128)} async-done(((f32[2,256,128]{2,1,0:T(8,128)}), f32[32,256,128]{2,1,0:T(8,128)}) %all-gather.7.cloned.1.call-update) | async-done | bytes 4194320 | tf_op jit(solution)/shard_map/all_gather | solution.py:26
  418.0 19.1 %while.27 = (s32[]{:T(128)}, f32[2,256,128]{2,1,0:T(8,128)S(1)}, s32[]{:T(128)}, f32[16,2,256,128]{3,2,1,0:T(8,128)}, f32[16,2,256,128]{3,2,1,0:T(8,128)}, /*index=5*/s32[]{:T(128)}, s32[]{:T(128)}) while((s32[]{:T(128)}, f32[2,256,128]{2,1,0:T(8,128)S(1)}, s32[]{:T(128)}, f32[16,2,256,128]{3,2,1,0:T(8,128)}, ...), condition=%wide.region_3.4_spmd.clone, body=%wide.region_2.3_spmd.clone.sunk | while | flops 262148 | bytes 1048685 | solution.py:35
  438.0 4.4 all-to-all-start.1
  442.4 14.8 %all-to-all-done.1 = f32[1,2,256,128]{3,1,0,2:T(2,128)S(1)} async-done(((f32[1,2,256,128]{3,1,0,2:T(2,128)}), f32[1,2,256,128]{3,1,0,2:T(2,128)S(1)}, u32[]{:S(2)}, u32[]{:S(2)}) %all-to-all-start.1) | async-done | bytes 262176 | tf_op jit(solution)/shard_map/all_to_all | solution.py:105
  (95 shorter events, 42.7 us)
Async XLA Ops:
  7.2 150.3 %copy-start = (s32[16,16,2]{1,2,0:T(2,128)S(1)}, s32[16,16,2]{1,2,0:T(2,128)}, u32[]{:S(2)}) copy-start(s32[16,16,2]{1,2,0:T(2,128)} %param.12) | copy-start | bytes 6148
  8.2 44.9 %collective-permute-start.3 = (f32[1,256,128]{2,1,0:T(8,128)S(1)}, f32[1,256,128]{2,1,0:T(8,128)S(1)}, u32[]{:S(2)}, u32[]{:S(2)}) collective-permute-start(f32[1,256,128]{2,1,0:T(8,128)S(1)} %get-tuple-element.209), channel_id=1, source_target_pairs={{0,1},{1,2},{2,3},{3,4},{4,5},{5,6},{6,7},{7,8},{8,9},{9,10},{10,1... | collective-permute-start | bytes 393224 | tf_op jit(solution)/shard_map/ppermute | solution.py:16
  31.3 32.5 %all-to-all-start = ((f32[16,1,2,16,128]{4,3,2,1,0:T(8,128)}), f32[16,1,2,16,128]{4,3,2,1,0:T(8,128)S(1)}, u32[]{:S(2)}, u32[]{:S(2)}) async-start(f32[16,1,2,16,128]{4,3,2,1,0:T(8,128)} %constant_dynamic-update-slice_fusion), calls=%async_computation | async-start | bytes 524288 | tf_op jit(solution)/shard_map/all_to_all | solution.py:78
  46.9 240.7 %all-gather.5.cloned.1.call-start = ((), (), s32[]{:S(2)}) async-start(), calls=%async_computation.3 | async-start | bytes 4456448 | tf_op jit(solution)/shard_map/all_gather | solution.py:26
  47.0 10.5 %collective-permute-start.2 = (f32[1,256,128]{2,1,0:T(8,128)S(1)}, f32[1,256,128]{2,1,0:T(8,128)S(1)}, u32[]{:S(2)}, u32[]{:S(2)}) collective-permute-start(f32[1,256,128]{2,1,0:T(8,128)S(1)} %get-tuple-element.210), channel_id=1, source_target_pairs={{1,0},{2,1},{3,2},{4,3},{5,4},{6,5},{7,6},{8,7},{9,8},{10,9},{11,1... | collective-permute-start | bytes 393224 | tf_op jit(solution)/shard_map/ppermute | solution.py:19
  63.8 92.0 %copy-start.3 = (f32[2,256,128]{2,1,0:T(8,128)S(1)}, f32[2,256,128]{2,1,0:T(8,128)}, u32[]{:S(2)}) copy-start(f32[2,256,128]{2,1,0:T(8,128)} %param.11) | copy-start | bytes 786436
  63.9 94.1 %copy-start.4 = (s32[16,16]{1,0:T(8,128)S(1)}, s32[16,16]{1,0:T(8,128)}, u32[]{:S(2)}) copy-start(s32[16,16]{1,0:T(8,128)} %param.13) | copy-start | bytes 3076
  63.9 9.2 %collective-permute-start = (f32[1,256,128]{2,1,0:T(8,128)S(1)}, f32[1,256,128]{2,1,0:T(8,128)S(1)}, u32[]{:S(2)}, u32[]{:S(2)}) collective-permute-start(f32[1,256,128]{2,1,0:T(8,128)S(1)} %get-tuple-element.270), channel_id=1, source_target_pairs={{0,1},{1,2},{2,3},{3,4},{4,5},{5,6},{6,7},{7,8},{8,9},{9,10},{10,1... | collective-permute-start | bytes 393224 | tf_op jit(solution)/shard_map/while/body/eval_jaxpr/ppermute | solution.py:16
  66.7 8.2 %collective-permute-start.1 = (f32[1,256,128]{2,1,0:T(8,128)S(1)}, f32[1,256,128]{2,1,0:T(8,128)S(1)}, u32[]{:S(2)}, u32[]{:S(2)}) collective-permute-start(f32[1,256,128]{2,1,0:T(8,128)S(1)} %get-tuple-element.271), channel_id=1, source_target_pairs={{1,0},{2,1},{3,2},{4,3},{5,4},{6,5},{7,6},{8,7},{9,8},{10,9},{11,1... | collective-permute-start | bytes 393224 | tf_op jit(solution)/shard_map/while/body/eval_jaxpr/ppermute | solution.py:19
  75.2 9.2 %collective-permute-start = (f32[1,256,128]{2,1,0:T(8,128)S(1)}, f32[1,256,128]{2,1,0:T(8,128)S(1)}, u32[]{:S(2)}, u32[]{:S(2)}) collective-permute-start(f32[1,256,128]{2,1,0:T(8,128)S(1)} %get-tuple-element.270), channel_id=1, source_target_pairs={{0,1},{1,2},{2,3},{3,4},{4,5},{5,6},{6,7},{7,8},{8,9},{9,10},{10,1... | collective-permute-start | bytes 393224 | tf_op jit(solution)/shard_map/while/body/eval_jaxpr/ppermute | solution.py:16
  77.1 9.0 %collective-permute-start.1 = (f32[1,256,128]{2,1,0:T(8,128)S(1)}, f32[1,256,128]{2,1,0:T(8,128)S(1)}, u32[]{:S(2)}, u32[]{:S(2)}) collective-permute-start(f32[1,256,128]{2,1,0:T(8,128)S(1)} %get-tuple-element.271), channel_id=1, source_target_pairs={{1,0},{2,1},{3,2},{4,3},{5,4},{6,5},{7,6},{8,7},{9,8},{10,9},{11,1... | collective-permute-start | bytes 393224 | tf_op jit(solution)/shard_map/while/body/eval_jaxpr/ppermute | solution.py:19
  86.5 9.3 %collective-permute-start = (f32[1,256,128]{2,1,0:T(8,128)S(1)}, f32[1,256,128]{2,1,0:T(8,128)S(1)}, u32[]{:S(2)}, u32[]{:S(2)}) collective-permute-start(f32[1,256,128]{2,1,0:T(8,128)S(1)} %get-tuple-element.270), channel_id=1, source_target_pairs={{0,1},{1,2},{2,3},{3,4},{4,5},{5,6},{6,7},{7,8},{8,9},{9,10},{10,1... | collective-permute-start | bytes 393224 | tf_op jit(solution)/shard_map/while/body/eval_jaxpr/ppermute | solution.py:16
  88.5 9.3 %collective-permute-start.1 = (f32[1,256,128]{2,1,0:T(8,128)S(1)}, f32[1,256,128]{2,1,0:T(8,128)S(1)}, u32[]{:S(2)}, u32[]{:S(2)}) collective-permute-start(f32[1,256,128]{2,1,0:T(8,128)S(1)} %get-tuple-element.271), channel_id=1, source_target_pairs={{1,0},{2,1},{3,2},{4,3},{5,4},{6,5},{7,6},{8,7},{9,8},{10,9},{11,1... | collective-permute-start | bytes 393224 | tf_op jit(solution)/shard_map/while/body/eval_jaxpr/ppermute | solution.py:19
  98.1 9.2 %collective-permute-start = (f32[1,256,128]{2,1,0:T(8,128)S(1)}, f32[1,256,128]{2,1,0:T(8,128)S(1)}, u32[]{:S(2)}, u32[]{:S(2)}) collective-permute-start(f32[1,256,128]{2,1,0:T(8,128)S(1)} %get-tuple-element.270), channel_id=1, source_target_pairs={{0,1},{1,2},{2,3},{3,4},{4,5},{5,6},{6,7},{7,8},{8,9},{9,10},{10,1... | collective-permute-start | bytes 393224 | tf_op jit(solution)/shard_map/while/body/eval_jaxpr/ppermute | solution.py:16
  100.1 9.1 %collective-permute-start.1 = (f32[1,256,128]{2,1,0:T(8,128)S(1)}, f32[1,256,128]{2,1,0:T(8,128)S(1)}, u32[]{:S(2)}, u32[]{:S(2)}) collective-permute-start(f32[1,256,128]{2,1,0:T(8,128)S(1)} %get-tuple-element.271), channel_id=1, source_target_pairs={{1,0},{2,1},{3,2},{4,3},{5,4},{6,5},{7,6},{8,7},{9,8},{10,9},{11,1... | collective-permute-start | bytes 393224 | tf_op jit(solution)/shard_map/while/body/eval_jaxpr/ppermute | solution.py:19
  109.5 9.2 %collective-permute-start = (f32[1,256,128]{2,1,0:T(8,128)S(1)}, f32[1,256,128]{2,1,0:T(8,128)S(1)}, u32[]{:S(2)}, u32[]{:S(2)}) collective-permute-start(f32[1,256,128]{2,1,0:T(8,128)S(1)} %get-tuple-element.270), channel_id=1, source_target_pairs={{0,1},{1,2},{2,3},{3,4},{4,5},{5,6},{6,7},{7,8},{8,9},{9,10},{10,1... | collective-permute-start | bytes 393224 | tf_op jit(solution)/shard_map/while/body/eval_jaxpr/ppermute | solution.py:16
  111.4 9.9 %collective-permute-start.1 = (f32[1,256,128]{2,1,0:T(8,128)S(1)}, f32[1,256,128]{2,1,0:T(8,128)S(1)}, u32[]{:S(2)}, u32[]{:S(2)}) collective-permute-start(f32[1,256,128]{2,1,0:T(8,128)S(1)} %get-tuple-element.271), channel_id=1, source_target_pairs={{1,0},{2,1},{3,2},{4,3},{5,4},{6,5},{7,6},{8,7},{9,8},{10,9},{11,1... | collective-permute-start | bytes 393224 | tf_op jit(solution)/shard_map/while/body/eval_jaxpr/ppermute | solution.py:19
  121.7 9.3 %collective-permute-start = (f32[1,256,128]{2,1,0:T(8,128)S(1)}, f32[1,256,128]{2,1,0:T(8,128)S(1)}, u32[]{:S(2)}, u32[]{:S(2)}) collective-permute-start(f32[1,256,128]{2,1,0:T(8,128)S(1)} %get-tuple-element.270), channel_id=1, source_target_pairs={{0,1},{1,2},{2,3},{3,4},{4,5},{5,6},{6,7},{7,8},{8,9},{9,10},{10,1... | collective-permute-start | bytes 393224 | tf_op jit(solution)/shard_map/while/body/eval_jaxpr/ppermute | solution.py:16
  123.7 9.1 %collective-permute-start.1 = (f32[1,256,128]{2,1,0:T(8,128)S(1)}, f32[1,256,128]{2,1,0:T(8,128)S(1)}, u32[]{:S(2)}, u32[]{:S(2)}) collective-permute-start(f32[1,256,128]{2,1,0:T(8,128)S(1)} %get-tuple-element.271), channel_id=1, source_target_pairs={{1,0},{2,1},{3,2},{4,3},{5,4},{6,5},{7,6},{8,7},{9,8},{10,9},{11,1... | collective-permute-start | bytes 393224 | tf_op jit(solution)/shard_map/while/body/eval_jaxpr/ppermute | solution.py:19
  133.2 9.3 %collective-permute-start = (f32[1,256,128]{2,1,0:T(8,128)S(1)}, f32[1,256,128]{2,1,0:T(8,128)S(1)}, u32[]{:S(2)}, u32[]{:S(2)}) collective-permute-start(f32[1,256,128]{2,1,0:T(8,128)S(1)} %get-tuple-element.270), channel_id=1, source_target_pairs={{0,1},{1,2},{2,3},{3,4},{4,5},{5,6},{6,7},{7,8},{8,9},{9,10},{10,1... | collective-permute-start | bytes 393224 | tf_op jit(solution)/shard_map/while/body/eval_jaxpr/ppermute | solution.py:16
  135.1 9.1 %collective-permute-start.1 = (f32[1,256,128]{2,1,0:T(8,128)S(1)}, f32[1,256,128]{2,1,0:T(8,128)S(1)}, u32[]{:S(2)}, u32[]{:S(2)}) collective-permute-start(f32[1,256,128]{2,1,0:T(8,128)S(1)} %get-tuple-element.271), channel_id=1, source_target_pairs={{1,0},{2,1},{3,2},{4,3},{5,4},{6,5},{7,6},{8,7},{9,8},{10,9},{11,1... | collective-permute-start | bytes 393224 | tf_op jit(solution)/shard_map/while/body/eval_jaxpr/ppermute | solution.py:19
  144.5 9.3 %collective-permute-start = (f32[1,256,128]{2,1,0:T(8,128)S(1)}, f32[1,256,128]{2,1,0:T(8,128)S(1)}, u32[]{:S(2)}, u32[]{:S(2)}) collective-permute-start(f32[1,256,128]{2,1,0:T(8,128)S(1)} %get-tuple-element.270), channel_id=1, source_target_pairs={{0,1},{1,2},{2,3},{3,4},{4,5},{5,6},{6,7},{7,8},{8,9},{9,10},{10,1... | collective-permute-start | bytes 393224 | tf_op jit(solution)/shard_map/while/body/eval_jaxpr/ppermute | solution.py:16
  146.5 9.0 %collective-permute-start.1 = (f32[1,256,128]{2,1,0:T(8,128)S(1)}, f32[1,256,128]{2,1,0:T(8,128)S(1)}, u32[]{:S(2)}, u32[]{:S(2)}) collective-permute-start(f32[1,256,128]{2,1,0:T(8,128)S(1)} %get-tuple-element.271), channel_id=1, source_target_pairs={{1,0},{2,1},{3,2},{4,3},{5,4},{6,5},{7,6},{8,7},{9,8},{10,9},{11,1... | collective-permute-start | bytes 393224 | tf_op jit(solution)/shard_map/while/body/eval_jaxpr/ppermute | solution.py:19
  156.7 280.4 %copy-start.1 = (f32[2,256,128]{2,1,0:T(8,128)S(1)}, f32[2,256,128]{2,1,0:T(8,128)}, u32[]{:S(2)}) copy-start(f32[2,256,128]{2,1,0:T(8,128)} %get-tuple-element.207) | copy-start | bytes 786436
  156.7 280.4 %copy-start.2 = (f32[2,256,128]{2,1,0:T(8,128)S(1)}, f32[2,256,128]{2,1,0:T(8,128)}, u32[]{:S(2)}) copy-start(f32[2,256,128]{2,1,0:T(8,128)} %get-tuple-element.208) | copy-start | bytes 786436
  156.7 261.3 %all-gather.7.cloned.1.call-start = ((), (), s32[]{:S(2)}) async-start(), calls=%async_computation.4 | async-start | bytes 4456448 | tf_op jit(solution)/shard_map/all_gather | solution.py:26
  159.7 278.3 %all-to-all-start.2 = ((f32[16,2,2,4,128]{4,3,2,1,0:T(4,128)}), f32[16,2,2,4,128]{4,3,2,1,0:T(4,128)S(1)}, u32[]{:S(2)}, u32[]{:S(2)}) async-start(f32[16,2,2,4,128]{4,3,2,1,0:T(4,128)} %select_select_fusion), calls=%async_computation.2 | async-start | bytes 262144 | tf_op jit(solution)/shard_map/all_to_all | solution.py:97
  438.0 19.2 %all-to-all-start.1 = ((f32[1,2,256,128]{3,1,0,2:T(2,128)}), f32[1,2,256,128]{3,1,0,2:T(2,128)S(1)}, u32[]{:S(2)}, u32[]{:S(2)}) async-start(f32[1,2,256,128]{3,1,0,2:T(2,128)} %copy.19), calls=%async_computation.1 | async-start | bytes 524288 | tf_op jit(solution)/shard_map/all_to_all | solution.py:105
Sparse Core Ops, SparseCore 0:
  156.8 130.7 all-gather.4
  290.8 127.1 all-gather.6
